TPU v7x, 32 devices: a whole 2x2x4 slice. The times are simulated.
32 devices in a mesh: space: 8 (over z, x), snap: 4 (over y, core).
Axes of the slice: x: 2, y: 2, z: 4, core: 2. Of those that a mesh axis runs over, the one named last changes fastest.
Arguments:
- snapshots: bfloat16 [131072, 512], P('space', 'snap'), may hold values from -6 to 6
- mass_blocks: bfloat16 [1024, 3, 128, 128], P(('space', 'snap')), may hold values from -0.3125 to 0.3125
- neighbours: int32 [1024, 3], P(('space', 'snap')), may hold values from 0 to 1023, as said below
- eigvecs: bfloat16 [512, 128], replicated, may hold values from -0.25 to 0.25
Outputs:
- weighted: bfloat16 [131072, 512], P(('space', 'snap'))
- correlation: float32 [512, 512], P('snap', 'space')
- modes: bfloat16 [131072, 128], P(('space', 'snap'))
Inputs may be any that keep to these rules, and one draw needn't show every extreme that they name: neighbours[b, 0] is b; every entry lies within 4 of b; neighbours[b, 2] lies exactly 4 away from b.
All inputs are finite; a program needn't handle non-finite values.
Results may differ from a plain program's by a relative error of at most 0.0029.
Values may be sent and summed in bfloat16 or wider, within the bound.
A program may use at most 128 MiB of HBM per device.

v0:
```python
import functools

import jax
import jax.numpy as jnp
from jax import lax
from jax.experimental import pallas as pl
from jax.experimental.pallas import tpu as pltpu
from jax.sharding import PartitionSpec as P

HB = 4
MESH = pl.DeviceIdType.MESH
BF16 = jnp.bfloat16
F32 = jnp.float32


def reduce_tiles(n, ns, part, recv1, send2, recv2, send3, recv3, send4, recv4,
                 s1, r1, s2, r2, s3, r3, s4, r4):
    ny, nz = n // 2, ns // 2
    s, k = lax.axis_index("space"), lax.axis_index("snap")
    y, c, z, x = k // 2, k % 2, s // 2, s % 2
    xo = 1 - x

    def remote(origin, target, sends, recvs, device):
        copy = pltpu.make_async_remote_copy(src_ref=origin, dst_ref=target, send_sem=sends,
                                            recv_sem=recvs, device_id=device, device_id_type=MESH)
        copy.start()
        return copy

    order = [lax.rem(y + t, ny) for t in range(1, ny)] + [y]
    first = [[remote(part.at[2 * yo + 1 - c, :, half], recv1.at[i, h], s1.at[i, h], r1.at[i, h],
                     (s, 2 * y + 1 - c)) for h, half in enumerate((xo, x))] for i, yo in enumerate(order)]
    second = []
    for i, yo in enumerate(order[:-1]):
        for h, half in enumerate((xo, x)):
            first[i][h].wait()
            send2[i, h] = part[2 * yo + c, :, half] + recv1[i, h]
            second.append((i, h, remote(send2.at[i, h], recv2.at[i, h], s2.at[i, h], r2.at[i, h],
                                        (s, 2 * yo + c))))

    def gathered(h, half):
        first[ny - 1][h].wait()
        value = part[2 * y + c, :, half] + recv1[ny - 1, h]
        for i, g, copy in second:
            if g == h:
                copy.wait()
                value = value + recv2[i, h]
        return value

    send3[...] = gathered(0, xo)
    third = remote(send3, recv3, s3, r3, (2 * z + xo, k))
    kept = gathered(1, x)
    third.wait()
    send4[...] = kept + recv3[...]
    last = []
    for t in range(1, nz):
        zo = lax.rem(z + t, nz)
        last.append(remote(send4.at[zo], recv4.at[t - 1], s4.at[t - 1], r4.at[t - 1], (2 * zo + x, k)))
    value = send4[z]
    for i, copy in enumerate(last):
        copy.wait()
        value = value + recv4[i]
    return value


def fused(n, ns, size, scale, near, src, mass_hbm, eig, weighted_hbm, modes_hbm, corr_out,
          ext, win, mass, weighted, modes, part, loc, own_sems, out_sems,
          send_mid, recv_mid, send_main, recv_main, send_fwd, recv_fwd,
          send_rim, recv_rim, send_out, *reduce_refs):
    ny, nz = n // 2, ns // 2
    s, k = lax.axis_index("space"), lax.axis_index("snap")
    y, c, z, x = k // 2, k % 2, s // 2, s % 2
    partner = 2 * y + 1 - c
    rim = HB * size
    total = src.shape[0]
    chip_rows = total // ny
    rows = chip_rows // 2
    pieces = rows // rim
    width = src.shape[1]

    barrier = pltpu.get_barrier_semaphore()
    for t in range(1, n):
        pl.semaphore_signal(barrier, inc=1, device_id=(s, lax.rem(k + t, n)), device_id_type=MESH)
    for t in range(1, nz):
        pl.semaphore_signal(barrier, inc=1, device_id=(2 * lax.rem(z + t, nz) + x, k), device_id_type=MESH)

    @pl.when(s > 0)
    def _():
        for t in range(n):
            pl.semaphore_signal(barrier, inc=1, device_id=(s - 1, t), device_id_type=MESH)

    @pl.when(s < ns - 1)
    def _():
        for t in range(n):
            pl.semaphore_signal(barrier, inc=1, device_id=(s + 1, t), device_id_type=MESH)

    def rows_of(first, count):
        return src.at[pl.ds(first, count)]

    keep = pltpu.make_async_copy(rows_of(y * chip_rows + c * (rows - rim), rows + rim),
                                 ext.at[k, pl.ds((1 - c) * rim, rows + rim)], loc.at[0])
    keep.start()
    inner = (k > 0) & (k < n - 1)
    edge_row = jnp.where(inner, jnp.where(c == 0, y * chip_rows - rim, (y + 1) * chip_rows), 0)
    edge_keep = pltpu.make_async_copy(rows_of(edge_row, rim), ext.at[k, pl.ds(c * (rows + rim), rim)],
                                      loc.at[1])
    pl.when(inner)(edge_keep.start)
    fetch = pltpu.make_async_copy(mass_hbm, mass, loc.at[2])
    fetch.start()
    part[...] = jnp.zeros_like(part)

    sides = jnp.where(s > 0, 1, 0) + jnp.where(s < ns - 1, 1, 0)
    pl.semaphore_wait(barrier, n - 1 + nz - 1 + n * sides)

    def remote(origin, slab, to_row, count, sends, recvs, device):
        return pltpu.make_async_remote_copy(
            src_ref=origin, dst_ref=ext.at[slab, pl.ds(to_row, count)],
            send_sem=sends, recv_sem=recvs, device_id=device, device_id_type=MESH)

    mids, mains = [], []
    for t in range(1, ny):
        yo = lax.rem(y + t, ny)
        base = yo * chip_rows
        for co in range(2):
            mids.append(remote(rows_of(base + rows - rim + co * rim, rim), k, rows if co == 0 else rim, rim,
                               send_mid.at[t, co], recv_mid.at[t, c], (s, 2 * yo + co)))
    for p in range(pieces - 1):
        for t in range(1, ny):
            yo = lax.rem(y + t, ny)
            base = yo * chip_rows
            for co in range(2):
                first = (pieces - 2 - p) * rim if co == 0 else rows + (1 + p) * rim
                to = (pieces - 1 - p) * rim if co == 0 else (2 + p) * rim
                mains.append(remote(rows_of(base + first, rim), k, to, rim, send_main.at[t, co, p],
                                    recv_main.at[t, c, p], (s, 2 * yo + co)))
    own = remote(rows_of(y * chip_rows + (1 - c) * (rows - rim), rows + rim), k, c * rim, rows + rim,
                 own_sems.at[0], own_sems.at[1], (s, partner))
    down = remote(rows_of(0, rim), k, rows + rim, rim, send_out.at[0], recv_rim.at[k], (s - 1, n - 1))
    up = remote(rows_of(total - rim, rim), k, 0, rim, send_out.at[1], recv_rim.at[k], (s + 1, 0))

    for copy in mids:
        copy.start()
    own.start()
    pl.when(s > 0)(down.start)
    pl.when(s < ns - 1)(up.start)
    edges = []
    for target in range(1, n - 1):
        low = target % 2 == 0
        first = (target // 2) * chip_rows - rim if low else (target // 2 + 1) * chip_rows
        edge = remote(rows_of(first, rim), k, 0 if low else rows + rim, rim,
                      send_rim.at[target], recv_rim.at[k], (s, target))
        edges.append((target, edge))
        pl.when(k != target)(edge.start)
    for copy in mains:
        copy.start()

    def wait_for(slab, to_row, count, recvs):
        remote(ext.at[slab, pl.ds(to_row, count)], slab, to_row, count, own_sems.at[0], recvs,
               (s, partner)).wait_recv()

    forwards = []
    at, to = (1 - c) * rows + c * rim, (1 - c) * (rows + rim)
    for t in range(1, ny):
        for co in range(2):
            slab = 2 * lax.rem(y + ny - t, ny) + co
            wait_for(slab, at, rim, recv_mid.at[t, co])
            forward = remote(ext.at[slab, pl.ds(at, rim)], slab, c * (rows + rim), rim,
                             send_fwd.at[t, co], recv_fwd.at[t, co], (s, partner))
            forward.start()
            forwards.append((slab, t, co, forward))
    keep.wait()
    wait_for(partner, (1 - c) * rim, rows + rim, own_sems.at[1])
    for slab, t, co, forward in forwards:
        wait_for(slab, to, rim, recv_fwd.at[t, co])
    fetch.wait()

    def slot_of(order):
        return jnp.where(c == 1, order, pieces + 1 - order)

    def admit(order):
        slot = slot_of(order)
        place = lax.rem(slot, 3) * HB
        for slab in range(n):
            held = ext[slab, pl.ds(pl.multiple_of(slot * rim, rim), rim), :]
            win[pl.ds(place, HB), :, slab * width:(slab + 1) * width] = held.reshape(HB, size, width)

    def out_copies(group):
        first = pl.multiple_of((slot_of(group + 1) - 1) * rim, rim)
        return [pltpu.make_async_copy(held.at[pl.ds(first, rim)], target.at[pl.ds(first, rim)],
                                      out_sems.at[i, group])
                for i, (held, target) in enumerate(((weighted, weighted_hbm), (modes, modes_hbm)))]

    def work(group):
        slot = slot_of(group + 1)
        first = pl.multiple_of((slot - 1) * rim, rim)
        for i in range(HB):
            row = (slot - 1) * HB + i
            masses = jnp.concatenate([mass[row, j] for j in range(mass.shape[1])], axis=1)
            fields = jnp.concatenate(
                [win[near[row, j]] for j in range(mass.shape[1])], axis=0)
            product = jnp.dot(masses, fields, preferred_element_type=F32)
            weighted[pl.ds(pl.multiple_of(first + i * size, size), size), :] = product.astype(BF16)
        here = win[pl.ds(lax.rem(slot, 3) * HB, HB)].reshape(rim, n * width)
        modes[pl.ds(first, rim), :] = jnp.dot(here, eig[...], preferred_element_type=F32).astype(BF16)
        sums = lax.dot_general(here, weighted[pl.ds(first, rim), :], (((0,), (0,)), ((), ())),
                               preferred_element_type=F32)
        tile = part.shape[3]
        for band in range(n):
            for index in range(ns):
                part[band, index // 2, index % 2] += sums[index * tile:(index + 1) * tile,
                                                          band * width:(band + 1) * width]
        for copy in out_copies(group):
            copy.start()

    admit(0)
    admit(1)

    @pl.loop(0, pieces - 1)
    def _(p):
        place = pl.multiple_of(slot_of(p + 2) * rim, rim)
        for slab, t, co, forward in forwards:
            wait_for(slab, place, rim, recv_main.at[t, co, p])
        admit(p + 2)
        work(p)

    lowest = (k == 0) & (s == 0)
    highest = (k == n - 1) & (s == ns - 1)
    pl.when(inner)(edge_keep.wait)
    for slab in range(n):
        expected = jnp.logical_not(lowest | highest | (inner & (k == slab)))

        @pl.when(expected)
        def _(slab=slab):
            wait_for(slab, c * (rows + rim), rim, recv_rim.at[slab])
    admit(pieces + 1)
    work(pieces - 1)

    corr_out[...] = reduce_tiles(n, ns, part, *reduce_refs) * scale

    for copy in mids + mains + [own] + [entry[3] for entry in forwards]:
        copy.wait_send()
    pl.when(s > 0)(down.wait_send)
    pl.when(s < ns - 1)(up.wait_send)
    for target, edge in edges:
        pl.when(k != target)(edge.wait_send)

    @pl.loop(0, pieces)
    def _(group):
        for copy in out_copies(group):
            copy.wait()


def fast_shards(n, ns, snapshots, mass_blocks, neighbours, eigvecs):
    block_rows, picks, size, _ = mass_blocks.shape
    total, width = snapshots.shape
    rim = HB * size
    rows = total // n
    snaps = n * width
    pieces = rows // rim
    sem = pltpu.SemaphoreType.DMA
    vmem = pltpu.VMEM
    ny, nz = n // 2, ns // 2
    tile = snaps // ns
    piece = (nz, tile, width)
    first_block = (lax.axis_index("space") * n + lax.axis_index("snap")) * block_rows
    near = lax.rem(neighbours - first_block + HB, 3 * HB)
    modes_count = eigvecs.shape[1]
    anywhere = pl.BlockSpec(memory_space=pl.ANY)
    weighted, modes, corr = pl.pallas_call(
        functools.partial(fused, n, ns, size, 1.0 / (total * ns)),
        out_shape=(jax.ShapeDtypeStruct((rows, snaps), BF16),
                   jax.ShapeDtypeStruct((rows, modes_count), BF16),
                   jax.ShapeDtypeStruct((tile, width), F32)),
        in_specs=[pl.BlockSpec(memory_space=pltpu.SMEM), anywhere, anywhere,
                  pl.BlockSpec(memory_space=pltpu.VMEM)],
        out_specs=(anywhere, anywhere, pl.BlockSpec(memory_space=pltpu.VMEM)),
        scratch_shapes=[
            vmem((n, rows + 2 * rim, width), BF16), vmem((3 * HB, size, snaps), BF16),
            vmem(mass_blocks.shape, BF16), vmem((rows, snaps), BF16), vmem((rows, modes_count), BF16),
            vmem((n, nz, 2, tile, width), F32),
            sem((3,)), sem((2,)), sem((2, pieces)),
            sem((ny, 2)), sem((ny, 2)), sem((ny, 2, pieces - 1)), sem((ny, 2, pieces - 1)),
            sem((ny, 2)), sem((ny, 2)), sem((n,)), sem((n,)), sem((2,)),
            vmem((ny, 2) + piece, F32), vmem((ny, 2) + piece, F32), vmem((ny, 2) + piece, F32),
            vmem(piece, F32), vmem(piece, F32), vmem(piece, F32), vmem(piece, F32),
            sem((ny, 2)), sem((ny, 2)), sem((ny, 2)), sem((ny, 2)), sem, sem, sem((nz,)), sem((nz,)),
        ],
        compiler_params=pltpu.CompilerParams(collective_id=0, has_side_effects=True,
                                             vmem_limit_bytes=40 * 2**20),
        name="fused",
    )(near, pltpu.with_memory_space_constraint(snapshots, pltpu.HBM), pltpu.with_memory_space_constraint(mass_blocks, pltpu.HBM), eigvecs)
    return weighted, corr.T, modes


def shifted(block, axis, distance):
    devices = range(lax.axis_size(axis))
    route = [(i - distance, i) for i in devices if i - distance in devices]
    return lax.ppermute(block, axis, route)


def plain_shards(snapshots, mass_blocks, neighbours, eigvecs):
    local_rows = lax.all_to_all(snapshots, "snap", split_axis=0, concat_axis=1, tiled=True)
    row_count, col_count = local_rows.shape
    block_size = mass_blocks.shape[2]
    rim_rows = HB * block_size
    below_rim = shifted(local_rows[row_count - rim_rows :], ("space", "snap"), 1)
    above_rim = shifted(local_rows[:rim_rows], ("space", "snap"), -1)
    extended = jnp.concatenate([below_rim, local_rows, above_rim], axis=0).reshape(
        -1, block_size, col_count
    )
    first_block = lax.axis_index(("space", "snap")) * (row_count // block_size)
    local_ids = neighbours - first_block + HB
    nearby = extended[local_ids]
    weighted = jnp.einsum("bjrc,bjcs->brs", mass_blocks, nearby, preferred_element_type=jnp.float32)
    weighted = weighted.reshape(row_count, col_count).astype(jnp.bfloat16)
    partial_corr = jnp.dot(weighted.T, local_rows, preferred_element_type=jnp.float32)
    band = lax.psum_scatter(partial_corr, "snap", scatter_dimension=0, tiled=True)
    correlation = lax.psum_scatter(band, "space", scatter_dimension=1, tiled=True)
    cell_total = row_count * lax.axis_size("space") * lax.axis_size("snap")
    correlation = correlation * (1.0 / cell_total)
    modes = jnp.dot(local_rows, eigvecs, preferred_element_type=jnp.float32).astype(jnp.bfloat16)
    return (weighted, correlation, modes)


def solution(mesh):
    n, ns = mesh.shape["snap"], mesh.shape["space"]

    def shards(snapshots, mass_blocks, neighbours, eigvecs):
        width = snapshots.shape[1]
        rows = snapshots.shape[0] // n
        tile = n * width // ns
        rim = HB * mass_blocks.shape[2]
        whole = width % 128 == 0 and tile % 8 == 0 and n % 2 == 0 and ns % 2 == 0
        if whole and n > 2 and ns > 2 and rows % rim == 0 and rows > 2 * rim:
            return fast_shards(n, ns, snapshots, mass_blocks, neighbours, eigvecs)
        return plain_shards(snapshots, mass_blocks, neighbours, eigvecs)

    in_specs = (
        P("space", "snap"),
        P(("space", "snap"), None, None, None),
        P(("space", "snap"), None),
        P(),
    )
    out_specs = (P(("space", "snap"), None), P("snap", "space"), P(("space", "snap"), None))
    return jax.shard_map(shards, mesh=mesh, in_specs=in_specs, out_specs=out_specs, check_vma=False)
```

profile of v0, /device:TPU:0, one launch (start us, length us, event | category | flops | bytes accessed | tf_op | source)
XLA Modules:
  0.0 82.2 jit_solution(14242640841470701258)
XLA Ops:
  0.6 0.7 subtract_add_fusion
  1.3 0.1 copy.10
  1.4 0.0 copy-start
  1.4 0.9 %copy-done = bf16[512,128]{1,0:T(8,128)(2,1)S(1)} copy-done((bf16[512,128]{1,0:T(8,128)(2,1)S(1)}, bf16[512,128]{1,0:T(8,128)(2,1)}, u32[]{:S(2)}) %copy-start) | copy-done | bytes 131096
  2.3 76.3 %fused.1 = (bf16[4096,512]{1,0:T(8,128)(2,1)S(1)}, bf16[4096,128]{1,0:T(8,128)(2,1)S(1)}, f32[64,128]{1,0:T(8,128)S(1)}) custom-call(s32[32,3]{1,0:T(8,128)S(1)} %broadcast_remainder_fusion.near, bf16[16384,128]{1,0:T(8,128)(2,1)} %src.1, bf16[32,3,128,128]{3,2,1,0:T(8,128)(2,1)} %mass_hbm.1, bf16[512,128]{1,0:T(8,128)(2,1)S(1)} %copy-done), custom_call_target="tpu_custom_call" | custom-call | tf_op jit(solution)/shard_map/fused/pallas_call | solution.py:268
  78.6 2.0 %copy.15 = bf16[4096,512]{1,0:T(8,128)(2,1)} copy(bf16[4096,512]{1,0:T(8,128)(2,1)S(1)} %get-tuple-element.12) | data formatting | bytes 8388608
  80.6 0.6 copy.16
  81.3 1.0 %copy.17 = bf16[4096,128]{1,0:T(8,128)(2,1)} copy(bf16[4096,128]{1,0:T(8,128)(2,1)S(1)} %get-tuple-element.14) | data formatting | bytes 2097152
  (1 shorter events, 0.0 us)
Async XLA Ops:
  1.4 0.9 %copy-start = (bf16[512,128]{1,0:T(8,128)(2,1)S(1)}, bf16[512,128]{1,0:T(8,128)(2,1)}, u32[]{:S(2)}) copy-start(bf16[512,128]{1,0:T(8,128)(2,1)} %eig.1) | copy-start | bytes 393220
where the time goes:
time: 82.4 us; the launch traced here: 82.2 us
  Pallas kernels  76.3 us (93%)
  local copies, waits for them, and re-layouts  4.59 us (6%)
    pallas_call x1, Pallas kernels, fast_shards(): pl.pallas_call(functools.partial(fused, n, ns, size, 1.0 / (total * ns)),...  76.3 us
    unnamed x5, local copies, waits for them, and re-layouts  4.5 us

commit v1 on v0

v1 whole, which is shorter than its diff:
```python
import functools

import jax
import jax.numpy as jnp
from jax import lax
from jax.experimental import pallas as pl
from jax.experimental.pallas import tpu as pltpu
from jax.sharding import PartitionSpec as P

HB = 4
MESH = pl.DeviceIdType.MESH
BF16 = jnp.bfloat16
F32 = jnp.float32


def transposed_dot(left, right):
    return lax.dot_general(left, right, (((0,), (0,)), ((), ())), preferred_element_type=F32)


def fused(n, ns, scale, near_hbm, src, mass_hbm, eig_hbm, weighted, modes, corr_out,
          base, far, win, mass, eig, near, acc, tiles, recv,
          loc, send_own, recv_own, recv_rim, send_far, recv_far, send_out, fwd_sems, tile_sems,
          gate, sync):
    nz = ns // 2
    s, k = lax.axis_index("space"), lax.axis_index("snap")
    y, c, z, x = k // 2, k % 2, s // 2, s % 2
    yo = 1 - y
    partner = 2 * y + 1 - c
    blocks, size, width = src.shape
    own_blocks = blocks // n
    chip_blocks = 2 * own_blocks
    pieces = own_blocks // HB
    rim = HB * size
    picks = mass.shape[1]
    top = HB + own_blocks
    first_block = (s * n + k) * own_blocks - HB
    lanes_own = pl.multiple_of(2 * y * width, 2 * width)
    lanes_far = [pl.multiple_of((2 * yo + i) * width, width) for i in range(2)]

    def local(i, origin, target):
        return pltpu.make_async_copy(origin, target, loc.at[i])

    def remote(origin, target, sends, recvs, device):
        return pltpu.make_async_remote_copy(src_ref=origin, dst_ref=target, send_sem=sends,
                                            recv_sem=recvs, device_id=device, device_id_type=MESH)

    def rows_of(first, count):
        return src.at[pl.ds(first, count)]

    def greet(sem):
        for t in range(1, n):
            pl.semaphore_signal(sem, inc=1, device_id=(s, lax.rem(k + t, n)), device_id_type=MESH)
        pl.semaphore_signal(sem, inc=1, device_id=(2 * z + 1 - x, k), device_id_type=MESH)

        @pl.when(z > 0)
        def _():
            pl.semaphore_signal(sem, inc=1, device_id=(s - 2, k), device_id_type=MESH)

        @pl.when(z < nz - 1)
        def _():
            pl.semaphore_signal(sem, inc=1, device_id=(s + 2, k), device_id_type=MESH)

        pl.semaphore_wait(sem, n + jnp.where(z > 0, 1, 0) + jnp.where(z < nz - 1, 1, 0))

    edge = c != y
    outer = edge | ((y == 0) & (s > 0)) | ((y == 1) & (s < ns - 1))
    cross_rim = ((y == 0) & (s > 0)) | ((y == 1) & (s < ns - 1))
    plane_rim = ((y == 0) & (s < ns - 1)) | ((y == 1) & (s > 0))

    keep = local(0, rows_of(y * chip_blocks + c * (own_blocks - HB), own_blocks + HB),
                 base.at[c, pl.ds((1 - c) * HB, own_blocks + HB)])
    edge_rows = rows_of(chip_blocks - y * HB, HB)
    edge_keep = local(1, edge_rows, base.at[c, pl.ds(yo * top, HB)])
    fetch = local(2, mass_hbm, mass)
    fetch_eig = local(3, eig_hbm, eig)
    fetch_near = local(4, near_hbm, near)

    mains = []
    for o in range(pieces):
        for co in range(2):
            at = yo * chip_blocks + ((pieces - 1 - o) * HB if co == 0 else own_blocks + o * HB)
            to = (pieces - o) * HB if co == 0 else (1 + o) * HB
            mains.append(remote(rows_of(at, HB), far.at[c, pl.ds(to, HB)], send_far.at[co, o],
                                recv_far.at[c, o + 1], (s, 2 * yo + co)))
    cross_edge = remote(rows_of(chip_blocks - yo * HB, HB), far.at[c, pl.ds(y * top, HB)],
                        send_out.at[0], recv_far.at[c, pieces + 1], (s, 2 * yo + y))
    cross = remote(rows_of(y * (blocks - HB), HB), far.at[c, pl.ds(yo * top, HB)],
                   send_out.at[1], recv_far.at[c, pieces + 1], (s + 2 * y - 1, yo * (n - 1)))
    plane = remote(rows_of(yo * (blocks - HB), HB), base.at[c, pl.ds(y * top, HB)],
                   send_out.at[2], recv_rim.at[c], (s + 1 - 2 * y, y * (n - 1)))
    plane_edge = remote(edge_rows, base.at[c, pl.ds(yo * top, HB)], send_out.at[3], recv_rim.at[c],
                        (s, partner))
    own = remote(rows_of(y * chip_blocks + (1 - c) * (own_blocks - HB), own_blocks + HB),
                 base.at[c, pl.ds(c * HB, own_blocks + HB)], send_own, recv_own, (s, partner))

    keep.start()
    pl.when(edge)(edge_keep.start)
    fetch_near.start()
    fetch.start()
    fetch_eig.start()

    greet(pltpu.get_barrier_semaphore())

    @pl.when(c == 0)
    def _():
        for copy in mains:
            copy.start()
        cross_edge.start()

    own.start()
    pl.when(jnp.logical_not(edge))(plane_edge.start)
    acc[...] = jnp.zeros_like(acc)
    for i in range(nz + 1):
        greet(sync.at[i])
    pl.when(plane_rim)(plane.start)
    pl.when(cross_rim & (c == 0))(cross.start)

    def wait_rim(buffer, index, recvs):
        remote(buffer.at[index, pl.ds(0, HB)], buffer.at[index, pl.ds(0, HB)], send_own, recvs,
               (s, partner)).wait_recv()

    def masses_of(row):
        return jnp.concatenate([mass[row, j] for j in range(picks)], axis=1)

    def place_of(row, j):
        return jnp.clip(near[j, row] - first_block, 0, base.shape[1] - 1)

    me = s * n + k

    def send_block(j, i):
        column = 2 * y + j if j < 2 else 2 * yo + j - 2
        band = 2 * y + i if i < 2 else 2 * yo + i - 2
        value = acc[j * width:(j + 1) * width, i * width:(i + 1) * width].astype(BF16)
        tiles[i, j] = value.reshape(tiles.shape[2:])
        for half in range(2):
            target = 2 * column + half
            mine = (target == s) & (band == k)
            copy = remote(tiles.at[i, j, half], recv.at[me], tile_sems.at[0], tile_sems.at[1],
                          (target, band))
            pl.when(jnp.logical_not(mine))(copy.start)

            @pl.when(mine)
            def _():
                recv[me] = tiles[i, j, half]

    keep.wait()
    own.wait_recv()
    pl.when(edge)(edge_keep.wait)
    for i in range(2):
        @pl.when(outer & (jnp.logical_not(edge) | (c != i)))
        def _():
            wait_rim(base, i, recv_rim.at[i])
    fetch.wait()
    fetch_near.wait()

    def held(buffer, index, slot):
        return buffer[index, pl.ds(pl.multiple_of(slot * HB, HB), HB)].reshape(rim, width)

    def near_fields(slot):
        return jnp.concatenate([held(base, 0, slot), held(base, 1, slot)], axis=1)

    @pl.loop(0, pieces)
    def _(group):
        for i in range(HB):
            row = group * HB + i
            places = [place_of(row, j) for j in range(picks)]
            fields = jnp.concatenate(
                [jnp.concatenate([base[half, place] for place in places], axis=0) for half in range(2)],
                axis=1)
            product = jnp.dot(masses_of(row), fields, preferred_element_type=F32)
            weighted[pl.ds(pl.multiple_of(row * size, size), size), pl.ds(lanes_own, 2 * width)] = (
                product.astype(BF16))
        rows = pl.ds(pl.multiple_of(group * rim, rim), rim)
        acc[0:2 * width, 0:2 * width] += transposed_dot(
            near_fields(group + 1), weighted[rows, pl.ds(lanes_own, 2 * width)])

    for j in range(2):
        for i in range(2):
            send_block(j, i)
    fetch_eig.wait()

    def slot_of(order):
        return jnp.where(c == 1, order, pieces + 1 - order)

    def phase(index):
        lanes = lanes_far[index]
        known = (2 + index) * width

        def rows_at(order):
            return pl.ds(pl.multiple_of((slot_of(order) - 1) * rim, rim), rim)

        def admit(order):
            first = pl.multiple_of(slot_of(order) * HB, HB)
            win[pl.ds(first, HB)] = far[index, pl.ds(first, HB)]

        def gathered(order, count):
            slot = slot_of(order)
            parts = [held(base, 0, slot), held(base, 1, slot)]
            return jnp.concatenate(parts + [held(far, i, slot) for i in range(count)], axis=1)

        def meet(order):
            rows = rows_at(order)
            parts = [weighted[rows, pl.ds(lanes_own, 2 * width)]]
            parts += [weighted[rows, pl.ds(lanes_far[i], width)] for i in range(index)]
            earlier = jnp.concatenate(parts, axis=1) if index else parts[0]
            acc[known:known + width, 0:known] += transposed_dot(
                held(far, index, slot_of(order)), earlier)
            if index == 1:
                vectors = jnp.concatenate(
                    [eig[pl.ds(lanes_own, 2 * width)]] + [eig[pl.ds(lanes_far[i], width)] for i in range(2)],
                    axis=0)
                modes[rows, :] = jnp.dot(gathered(order, 2), vectors,
                                         preferred_element_type=F32).astype(BF16)

        def work(order):
            slot = slot_of(order)
            for i in range(HB):
                row = (slot - 1) * HB + i
                fields = jnp.concatenate([win[place_of(row, j)] for j in range(picks)], axis=0)
                product = jnp.dot(masses_of(row), fields, preferred_element_type=F32)
                weighted[pl.ds(pl.multiple_of(row * size, size), size), pl.ds(lanes, width)] = (
                    product.astype(BF16))
            acc[0:known + width, known:known + width] += transposed_dot(
                gathered(order, index + 1), weighted[rows_at(order), pl.ds(lanes, width)])

        wait_rim(far, index, recv_far.at[index, 1])
        mid = far.at[index, pl.ds(slot_of(1) * HB, HB)]
        forward = remote(mid, far.at[index, pl.ds(c * top, HB)], fwd_sems.at[index],
                         recv_far.at[index, 0], (s, partner))
        forward.start()
        admit(1)
        meet(1)
        wait_rim(far, index, recv_far.at[index, 0])
        admit(0)

        @pl.loop(0, pieces - 1)
        def _(p):
            wait_rim(far, index, recv_far.at[index, p + 2])
            admit(p + 2)
            meet(p + 2)
            if index == 0:
                ready = p == pieces - 3

                @pl.when(ready & (c == 0))
                def _():
                    for co in range(2):
                        mains[2 * (pieces - 4) + co].wait_send()
                    pl.semaphore_signal(gate, inc=1, device_id=(s, partner), device_id_type=MESH)

                @pl.when(ready & (c == 1))
                def _():
                    pl.semaphore_wait(gate, 1)
                    for copy in mains:
                        copy.start()
                    cross_edge.start()
                    pl.when(cross_rim)(cross.start)
            work(p + 1)

        for i in range(2 + index):
            send_block(2 + index, i)

        @pl.when(outer)
        def _():
            wait_rim(far, index, recv_far.at[index, pieces + 1])
        admit(pieces + 1)
        work(pieces)
        for j in range(3 + index):
            send_block(j, 2 + index)
        forward.wait_send()

    phase(0)
    phase(1)

    for i, copy in enumerate(mains):
        if i // 2 == pieces - 4:
            pl.when(c == 1)(copy.wait_send)
        else:
            copy.wait_send()
    cross_edge.wait_send()
    own.wait_send()
    pl.when(jnp.logical_not(edge))(plane_edge.wait_send)
    pl.when(plane_rim)(plane.wait_send)
    pl.when(cross_rim)(cross.wait_send)
    others = recv.at[pl.ds(0, n * ns - 1)]
    remote(others, others, tile_sems.at[0], tile_sems.at[1], (s, partner)).wait()
    total = recv[0].astype(F32)
    for i in range(1, n * ns):
        total = total + recv[i].astype(F32)
    corr_out[...] = total * scale


def deliver(weighted, modes, corr, weighted_out, modes_out, corr_out, sems):
    parts = sems.shape[0] // 2 - 1
    pairs = [(corr, corr_out)]
    for held, target in ((weighted, weighted_out), (modes, modes_out)):
        rows = held.shape[0] // parts
        pairs += [(held.at[pl.ds(i * rows, rows)], target.at[pl.ds(i * rows, rows)]) for i in range(parts)]
    copies = [pltpu.make_async_copy(held, target, sems.at[i]) for i, (held, target) in enumerate(pairs)]
    for copy in copies:
        copy.start()
    for copy in copies:
        copy.wait()


def fast_shards(n, ns, snapshots, mass_blocks, neighbours, eigvecs):
    own_blocks, picks, size, _ = mass_blocks.shape
    total, width = snapshots.shape
    rows = total // n
    snaps = n * width
    pieces = own_blocks // HB
    sem = pltpu.SemaphoreType.DMA
    regular = pltpu.SemaphoreType.REGULAR
    vmem = pltpu.VMEM
    nz = ns // 2
    tile = snaps // ns
    held = own_blocks + 2 * HB
    modes_count = eigvecs.shape[1]
    hbm = pl.BlockSpec(memory_space=pltpu.HBM)
    inside = pl.BlockSpec(memory_space=pltpu.VMEM)
    block = (size, width)
    weighted, modes, corr = pl.pallas_call(
        functools.partial(fused, n, ns, 1.0 / (total * ns)),
        out_shape=(jax.ShapeDtypeStruct((rows, snaps), BF16),
                   jax.ShapeDtypeStruct((rows, modes_count), BF16),
                   jax.ShapeDtypeStruct((tile, width), F32)),
        in_specs=[hbm] * 4,
        out_specs=(inside, inside, inside),
        scratch_shapes=[
            vmem((2, held) + block, BF16), vmem((2, held) + block, BF16), vmem((held,) + block, BF16),
            vmem(mass_blocks.shape, BF16), vmem(eigvecs.shape, BF16),
            pltpu.SMEM((picks, own_blocks), jnp.int32), vmem((snaps, snaps), F32),
            vmem((n, n, 2, tile, width), BF16), vmem((n * ns, tile, width), BF16),
            sem((5,)), sem, sem, sem((2,)), sem((2, pieces)), sem((2, pieces + 2)), sem((4,)), sem((2,)),
            sem((2,)), regular, regular((nz + 1,)),
        ],
        compiler_params=pltpu.CompilerParams(collective_id=0, has_side_effects=True,
                                             vmem_limit_bytes=40 * 2**20),
        name="fused",
    )(*(pltpu.with_memory_space_constraint(a, pltpu.HBM) for a in (
        neighbours.T, snapshots.reshape(total // size, size, width), mass_blocks, eigvecs)))
    weighted, modes, corr = pl.pallas_call(
        deliver,
        out_shape=tuple(pltpu.HBM(a.shape, a.dtype) for a in (weighted, modes, corr)),
        in_specs=[inside] * 3,
        out_specs=(hbm,) * 3,
        scratch_shapes=[sem((10,))],
        compiler_params=pltpu.CompilerParams(vmem_limit_bytes=2**20),
        name="deliver",
    )(*(pltpu.with_memory_space_constraint(a, pltpu.VMEM) for a in (weighted, modes, corr)))
    return weighted, corr.T, modes


def shifted(block, axis, distance):
    devices = range(lax.axis_size(axis))
    route = [(i - distance, i) for i in devices if i - distance in devices]
    return lax.ppermute(block, axis, route)


def plain_shards(snapshots, mass_blocks, neighbours, eigvecs):
    local_rows = lax.all_to_all(snapshots, "snap", split_axis=0, concat_axis=1, tiled=True)
    row_count, col_count = local_rows.shape
    block_size = mass_blocks.shape[2]
    rim_rows = HB * block_size
    below_rim = shifted(local_rows[row_count - rim_rows :], ("space", "snap"), 1)
    above_rim = shifted(local_rows[:rim_rows], ("space", "snap"), -1)
    extended = jnp.concatenate([below_rim, local_rows, above_rim], axis=0).reshape(
        -1, block_size, col_count
    )
    first_block = lax.axis_index(("space", "snap")) * (row_count // block_size)
    local_ids = neighbours - first_block + HB
    nearby = extended[local_ids]
    weighted = jnp.einsum("bjrc,bjcs->brs", mass_blocks, nearby, preferred_element_type=jnp.float32)
    weighted = weighted.reshape(row_count, col_count).astype(jnp.bfloat16)
    partial_corr = jnp.dot(weighted.T, local_rows, preferred_element_type=jnp.float32)
    band = lax.psum_scatter(partial_corr, "snap", scatter_dimension=0, tiled=True)
    correlation = lax.psum_scatter(band, "space", scatter_dimension=1, tiled=True)
    cell_total = row_count * lax.axis_size("space") * lax.axis_size("snap")
    correlation = correlation * (1.0 / cell_total)
    modes = jnp.dot(local_rows, eigvecs, preferred_element_type=jnp.float32).astype(jnp.bfloat16)
    return (weighted, correlation, modes)


def solution(mesh):
    n, ns = mesh.shape["snap"], mesh.shape["space"]

    def shards(snapshots, mass_blocks, neighbours, eigvecs):
        width = snapshots.shape[1]
        own_blocks, _, size, _ = mass_blocks.shape
        rows = own_blocks * size
        whole = n == 4 and ns == 2 * n and width % 128 == 0 and width == size
        if whole and snapshots.shape[0] == n * rows and own_blocks % HB == 0 and own_blocks >= 4 * HB:
            return fast_shards(n, ns, snapshots, mass_blocks, neighbours, eigvecs)
        return plain_shards(snapshots, mass_blocks, neighbours, eigvecs)

    in_specs = (
        P("space", "snap"),
        P(("space", "snap"), None, None, None),
        P(("space", "snap"), None),
        P(),
    )
    out_specs = (P(("space", "snap"), None), P("snap", "space"), P(("space", "snap"), None))
    return jax.shard_map(shards, mesh=mesh, in_specs=in_specs, out_specs=out_specs, check_vma=False)
```

time: 82.4 us -> 69.2 us (0.84)
  the two profiles are of different devices: /device:TPU:0 before, /device:TPU:1 now
where the time goes in v1:
time: 69.2 us; the launch traced here: 69.1 us
  Pallas kernels  68.4 us (99%)
    pallas_call x1, Pallas kernels, fast_shards(): pl.pallas_call(functools.partial(fused, n, ns, 1.0 / (total * ns)), out_s...  66 us
    pallas_call x1, Pallas kernels, fast_shards(): pl.pallas_call(deliver, out_shape=tuple((pltpu.HBM(a.shape, a.dtype) for...  2.42 us

profile of v1, /device:TPU:1, one launch (start us, length us, event | category | flops | bytes accessed | tf_op | source)
XLA Modules:
  0.0 69.1 jit_solution(5290150007680103413)
XLA Ops:
  0.6 66.0 %fused.1 = (bf16[4096,512]{1,0:T(8,128)(2,1)S(1)}, bf16[4096,128]{1,0:T(8,128)(2,1)S(1)}, f32[64,128]{1,0:T(8,128)S(1)}) custom-call(s32[3,32]{1,0:T(4,128)} %bitcast.4, bf16[128,128,128]{2,1,0:T(8,128)(2,1)} %bitcast.3, bf16[32,3,128,128]{3,2,1,0:T(8,128)(2,1)} %mass_hbm.1, bf16[512,128]{1,0:T(8,128)(2,1)} %eig_hbm.1), custom_call_target="tpu_custom_call" | custom-call | tf_op jit(solution)/shard_map/fused/pallas_call | solution.py:321
  66.7 2.4 %deliver.1 = (bf16[4096,512]{1,0:T(8,128)(2,1)}, bf16[4096,128]{1,0:T(8,128)(2,1)}, f32[64,128]{1,0:T(8,128)}) custom-call(bf16[4096,512]{1,0:T(8,128)(2,1)S(1)} %get-tuple-element.9.weighted, bf16[4096,128]{1,0:T(8,128)(2,1)S(1)} %get-tuple-element.10.modes, f32[64,128]{1,0:T(8,128)S(1)} %get-tuple-element.11.corr), custom_call_target="tpu_custom_call" | custom-call | tf_op jit(solution)/shard_map/deliver/pallas_call | solution.py:341

commit v2 on v1

--- a/solution.py
+++ b/solution.py
@@ -18,9 +18,9 @@
 
 
 def fused(n, ns, scale, near_hbm, src, mass_hbm, eig_hbm, weighted, modes, corr_out,
-          base, far, win, mass, eig, near, acc, tiles, recv,
-          loc, send_own, recv_own, recv_rim, send_far, recv_far, send_out, fwd_sems, tile_sems,
-          gate, sync):
+          base, far, win, mass, eig, near, acc, late, given, given_late, tiles, recv,
+          loc, send_own, recv_own, recv_rim, send_far, recv_far, send_out, fwd_sems, give_sems, take_sems,
+          tile_sems, gate, sync):
     nz = ns // 2
     s, k = lax.axis_index("space"), lax.axis_index("snap")
     y, c, z, x = k // 2, k % 2, s // 2, s % 2
@@ -47,7 +47,7 @@
     def rows_of(first, count):
         return src.at[pl.ds(first, count)]
 
-    def greet(sem):
+    def hail(sem):
         for t in range(1, n):
             pl.semaphore_signal(sem, inc=1, device_id=(s, lax.rem(k + t, n)), device_id_type=MESH)
         pl.semaphore_signal(sem, inc=1, device_id=(2 * z + 1 - x, k), device_id_type=MESH)
@@ -60,8 +60,11 @@
         def _():
             pl.semaphore_signal(sem, inc=1, device_id=(s + 2, k), device_id_type=MESH)
 
+    def heed(sem):
         pl.semaphore_wait(sem, n + jnp.where(z > 0, 1, 0) + jnp.where(z < nz - 1, 1, 0))
 
+    barrier = pltpu.get_barrier_semaphore()
+    hail(barrier)
     edge = c != y
     outer = edge | ((y == 0) & (s > 0)) | ((y == 1) & (s < ns - 1))
     cross_rim = ((y == 0) & (s > 0)) | ((y == 1) & (s < ns - 1))
@@ -80,8 +83,12 @@
         for co in range(2):
             at = yo * chip_blocks + ((pieces - 1 - o) * HB if co == 0 else own_blocks + o * HB)
             to = (pieces - o) * HB if co == 0 else (1 + o) * HB
-            mains.append(remote(rows_of(at, HB), far.at[c, pl.ds(to, HB)], send_far.at[co, o],
+            mains.append(remote(rows_of(at, HB), far.at[c, pl.ds(to, HB)], send_far.at[jnp.where((c == 0) & (o == pieces - 4), 1, 0)] if o == pieces - 4 else send_far.at[0],
                                 recv_far.at[c, o + 1], (s, 2 * yo + co)))
+    def sent(count, i):
+        rows = rows_of(0, count * HB)
+        remote(rows, rows, send_far.at[i], recv_own, (s, partner)).wait_send()
+
     cross_edge = remote(rows_of(chip_blocks - yo * HB, HB), far.at[c, pl.ds(y * top, HB)],
                         send_out.at[0], recv_far.at[c, pieces + 1], (s, 2 * yo + y))
     cross = remote(rows_of(y * (blocks - HB), HB), far.at[c, pl.ds(yo * top, HB)],
@@ -99,7 +106,9 @@
     fetch.start()
     fetch_eig.start()
 
-    greet(pltpu.get_barrier_semaphore())
+    acc[...] = jnp.zeros_like(acc)
+    late[...] = jnp.zeros_like(late)
+    heed(barrier)
 
     @pl.when(c == 0)
     def _():
@@ -109,9 +118,9 @@
 
     own.start()
     pl.when(jnp.logical_not(edge))(plane_edge.start)
-    acc[...] = jnp.zeros_like(acc)
     for i in range(nz + 1):
-        greet(sync.at[i])
+        hail(sync.at[i])
+        heed(sync.at[i])
     pl.when(plane_rim)(plane.start)
     pl.when(cross_rim & (c == 0))(cross.start)
 
@@ -125,23 +134,66 @@
     def place_of(row, j):
         return jnp.clip(near[j, row] - first_block, 0, base.shape[1] - 1)
 
-    me = s * n + k
-
-    def send_block(j, i):
-        column = 2 * y + j if j < 2 else 2 * yo + j - 2
-        band = 2 * y + i if i < 2 else 2 * yo + i - 2
-        value = acc[j * width:(j + 1) * width, i * width:(i + 1) * width].astype(BF16)
-        tiles[i, j] = value.reshape(tiles.shape[2:])
+    def span(first, last):
+        return pl.ds(first * width, (last - first) * width)
+
+    def give(kind, order, band, first, last):
+        rows = span(first, last)
+        return remote(acc.at[band, rows], given.at[kind, rows], give_sems.at[3 * kind + order],
+                      take_sems.at[3 * kind + order], (s, partner))
+
+    def column_of(j):
+        return 2 * y + j if j < 2 else 2 * yo + j - 2
+
+    def pack(kind, j, value):
+        tiles[kind, j] = value.astype(BF16).reshape(tiles.shape[2:])
+
+    def send_tiles(kind, j, slot, band):
         for half in range(2):
-            target = 2 * column + half
-            mine = (target == s) & (band == k)
-            copy = remote(tiles.at[i, j, half], recv.at[me], tile_sems.at[0], tile_sems.at[1],
+            target = 2 * column_of(j) + half
+            copy = remote(tiles.at[kind, j, half], recv.at[slot], tile_sems.at[0], tile_sems.at[1],
                           (target, band))
+            if kind:
+                copy.start()
+                continue
+            mine = target == s
             pl.when(jnp.logical_not(mine))(copy.start)
 
             @pl.when(mine)
             def _():
-                recv[me] = tiles[i, j, half]
+                recv[slot] = tiles[kind, j, half]
+
+    def share_own(order, first, last):
+        copy = give(0, order, 1 - c, first, last)
+        copy.start()
+
+        def finish():
+            copy.wait()
+            for j in range(first, last):
+                rows = span(j, j + 1)
+                pack(0, j, acc[c, rows] + given[0, rows])
+                send_tiles(0, j, s, k)
+
+        return finish
+
+    def give_far(order, first, last):
+        @pl.when(c == 0)
+        def _():
+            give(1, order, 2, first, last).start()
+
+    def pack_far_band(order, first, last):
+        @pl.when(c == 1)
+        def _():
+            give(1, order, 2, first, last).wait_recv()
+            for j in range(first, last):
+                rows = span(j, j + 1)
+                pack(1, j, acc[2, rows] + given[1, rows])
+
+    def send_far_band(first, last):
+        @pl.when(c == 1)
+        def _():
+            for j in range(first, last):
+                send_tiles(1, j, ns + s, 2 * yo)
 
     keep.wait()
     own.wait_recv()
@@ -155,6 +207,10 @@
 
     def held(buffer, index, slot):
         return buffer[index, pl.ds(pl.multiple_of(slot * HB, HB), HB)].reshape(rim, width)
+
+    def add(first, last, band, count, value):
+        for i in range(count):
+            acc[band + i, first * width:last * width] += value[:, i * width:(i + 1) * width]
 
     def near_fields(slot):
         return jnp.concatenate([held(base, 0, slot), held(base, 1, slot)], axis=1)
@@ -171,12 +227,9 @@
             weighted[pl.ds(pl.multiple_of(row * size, size), size), pl.ds(lanes_own, 2 * width)] = (
                 product.astype(BF16))
         rows = pl.ds(pl.multiple_of(group * rim, rim), rim)
-        acc[0:2 * width, 0:2 * width] += transposed_dot(
-            near_fields(group + 1), weighted[rows, pl.ds(lanes_own, 2 * width)])
-
-    for j in range(2):
-        for i in range(2):
-            send_block(j, i)
+        add(0, 2, 0, 2, transposed_dot(near_fields(group + 1), weighted[rows, pl.ds(lanes_own, 2 * width)]))
+
+    share_own(0, 0, 2)()
     fetch_eig.wait()
 
     def slot_of(order):
@@ -184,7 +237,7 @@
 
     def phase(index):
         lanes = lanes_far[index]
-        known = (2 + index) * width
+        known = 2 + index
 
         def rows_at(order):
             return pl.ds(pl.multiple_of((slot_of(order) - 1) * rim, rim), rim)
@@ -203,14 +256,14 @@
             parts = [weighted[rows, pl.ds(lanes_own, 2 * width)]]
             parts += [weighted[rows, pl.ds(lanes_far[i], width)] for i in range(index)]
             earlier = jnp.concatenate(parts, axis=1) if index else parts[0]
-            acc[known:known + width, 0:known] += transposed_dot(
-                held(far, index, slot_of(order)), earlier)
-            if index == 1:
-                vectors = jnp.concatenate(
-                    [eig[pl.ds(lanes_own, 2 * width)]] + [eig[pl.ds(lanes_far[i], width)] for i in range(2)],
-                    axis=0)
-                modes[rows, :] = jnp.dot(gathered(order, 2), vectors,
-                                         preferred_element_type=F32).astype(BF16)
+            add(known, known + 1, 0, known, transposed_dot(held(far, index, slot_of(order)), earlier))
+
+        def project(order):
+            vectors = jnp.concatenate(
+                [eig[pl.ds(lanes_own, 2 * width)]] + [eig[pl.ds(lanes_far[i], width)] for i in range(2)],
+                axis=0)
+            modes[rows_at(order), :] = jnp.dot(gathered(order, 2), vectors,
+                                               preferred_element_type=F32).astype(BF16)
 
         def work(order):
             slot = slot_of(order)
@@ -220,8 +273,8 @@
                 product = jnp.dot(masses_of(row), fields, preferred_element_type=F32)
                 weighted[pl.ds(pl.multiple_of(row * size, size), size), pl.ds(lanes, width)] = (
                     product.astype(BF16))
-            acc[0:known + width, known:known + width] += transposed_dot(
-                gathered(order, index + 1), weighted[rows_at(order), pl.ds(lanes, width)])
+            late[index, :, 0:(known + 1) * width] += transposed_dot(
+                weighted[rows_at(order), pl.ds(lanes, width)], gathered(order, index + 1))
 
         wait_rim(far, index, recv_far.at[index, 1])
         mid = far.at[index, pl.ds(slot_of(1) * HB, HB)]
@@ -230,71 +283,122 @@
         forward.start()
         admit(1)
         meet(1)
+        if index == 1:
+            project(1)
         wait_rim(far, index, recv_far.at[index, 0])
         admit(0)
 
-        @pl.loop(0, pieces - 1)
+        @pl.loop(0, pieces - 2)
         def _(p):
             wait_rim(far, index, recv_far.at[index, p + 2])
             admit(p + 2)
             meet(p + 2)
+            if index == 1:
+                project(p + 2)
             if index == 0:
                 ready = p == pieces - 3
 
                 @pl.when(ready & (c == 0))
                 def _():
-                    for co in range(2):
-                        mains[2 * (pieces - 4) + co].wait_send()
+                    sent(2, 1)
                     pl.semaphore_signal(gate, inc=1, device_id=(s, partner), device_id_type=MESH)
 
                 @pl.when(ready & (c == 1))
                 def _():
                     pl.semaphore_wait(gate, 1)
+                    pl.when(cross_rim)(cross.start)
                     for copy in mains:
                         copy.start()
                     cross_edge.start()
-                    pl.when(cross_rim)(cross.start)
             work(p + 1)
 
-        for i in range(2 + index):
-            send_block(2 + index, i)
-
-        @pl.when(outer)
+        wait_rim(far, index, recv_far.at[index, pieces])
+        if index == 1:
+            send_far_band(0, known)
+        admit(pieces)
+        meet(pieces)
+        finish = share_own(index + 1, known, known + 1)
+        if index == 1:
+            give_far(1, known, known + 1)
+        work(pieces - 1)
+
+        if index == 0:
+            finish()
+            pl.when(outer)(lambda: wait_rim(far, index, recv_far.at[index, pieces + 1]))
+            admit(pieces + 1)
+            work(pieces)
+            for j in range(known + 1):
+                acc[known, j * width:(j + 1) * width] = late[index, :, j * width:(j + 1) * width].T
+            give_far(0, 0, known + 1)
+            pack_far_band(0, 0, known + 1)
+            forward.wait_send()
+            return
+
+        last_give = remote(late.at[index], given_late, give_sems.at[5], take_sems.at[5], (s, partner))
+
+        @pl.when(jnp.logical_not(edge))
+        def _():
+            pl.when(outer)(lambda: wait_rim(far, index, recv_far.at[index, pieces + 1]))
+            admit(pieces + 1)
+            work(pieces)
+            last_give.start()
+
+        finish()
+        pack_far_band(1, known, known + 1)
+        send_far_band(known, known + 1)
+
+        @pl.when(edge)
         def _():
             wait_rim(far, index, recv_far.at[index, pieces + 1])
-        admit(pieces + 1)
-        work(pieces)
-        for j in range(3 + index):
-            send_block(j, 2 + index)
+            admit(pieces + 1)
+            work(pieces)
+            last_give.wait_recv()
+            for t in range(n):
+                column = jnp.where(z < n // 2, n - 1 - t, t)
+                j = lax.rem(column, 2) + jnp.where(column // 2 == y, 0, 2)
+                lanes_of = pl.ds(pl.multiple_of(j * width, width), width)
+                value = (late[index, :, lanes_of] + given_late[:, lanes_of]).T
+                tiles[2, t] = value.astype(BF16).reshape(tiles.shape[2:])
+                for half in range(2):
+                    remote(tiles.at[2, t, half], recv.at[ns + s], tile_sems.at[0], tile_sems.at[1],
+                           (2 * column + half, 2 * yo + 1)).start()
+
+        project(pieces)
         forward.wait_send()
+        pl.when(jnp.logical_not(edge))(last_give.wait_send)
 
     phase(0)
     phase(1)
 
-    for i, copy in enumerate(mains):
-        if i // 2 == pieces - 4:
-            pl.when(c == 1)(copy.wait_send)
-        else:
-            copy.wait_send()
+    pl.when(c == 0)(lambda: sent(2 * pieces - 2, 0))
+    pl.when(c == 1)(lambda: sent(2 * pieces, 0))
     cross_edge.wait_send()
     own.wait_send()
     pl.when(jnp.logical_not(edge))(plane_edge.wait_send)
     pl.when(plane_rim)(plane.wait_send)
     pl.when(cross_rim)(cross.wait_send)
-    others = recv.at[pl.ds(0, n * ns - 1)]
-    remote(others, others, tile_sems.at[0], tile_sems.at[1], (s, partner)).wait()
+    tile_bytes = remote(recv.at[pl.ds(0, ns)], recv.at[pl.ds(0, ns)], tile_sems.at[0], tile_sems.at[1],
+                        (s, partner))
+    own_tiles = recv.at[pl.ds(0, ns - 1)]
+    remote(own_tiles, own_tiles, tile_sems.at[0], tile_sems.at[1], (s, partner)).wait_send()
+
+    @pl.when(c == 0)
+    def _():
+        for order, first, last in ((0, 0, n - 1), (1, n - 1, n)):
+            give(1, order, 2, first, last).wait_send()
+
+    pl.when(c == 1)(tile_bytes.wait_send)
+    pl.when(edge)(tile_bytes.wait_send)
+    all_tiles = recv.at[pl.ds(0, 2 * ns - 1)]
+    remote(all_tiles, all_tiles, tile_sems.at[0], tile_sems.at[1], (s, partner)).wait_recv()
     total = recv[0].astype(F32)
-    for i in range(1, n * ns):
+    for i in range(1, 2 * ns):
         total = total + recv[i].astype(F32)
     corr_out[...] = total * scale
 
 
 def deliver(weighted, modes, corr, weighted_out, modes_out, corr_out, sems):
-    parts = sems.shape[0] // 2 - 1
-    pairs = [(corr, corr_out)]
-    for held, target in ((weighted, weighted_out), (modes, modes_out)):
-        rows = held.shape[0] // parts
-        pairs += [(held.at[pl.ds(i * rows, rows)], target.at[pl.ds(i * rows, rows)]) for i in range(parts)]
+    pairs = ((weighted, weighted_out), (modes, modes_out), (corr, corr_out))
     copies = [pltpu.make_async_copy(held, target, sems.at[i]) for i, (held, target) in enumerate(pairs)]
     for copy in copies:
         copy.start()
@@ -328,10 +432,11 @@
         scratch_shapes=[
             vmem((2, held) + block, BF16), vmem((2, held) + block, BF16), vmem((held,) + block, BF16),
             vmem(mass_blocks.shape, BF16), vmem(eigvecs.shape, BF16),
-            pltpu.SMEM((picks, own_blocks), jnp.int32), vmem((snaps, snaps), F32),
-            vmem((n, n, 2, tile, width), BF16), vmem((n * ns, tile, width), BF16),
-            sem((5,)), sem, sem, sem((2,)), sem((2, pieces)), sem((2, pieces + 2)), sem((4,)), sem((2,)),
-            sem((2,)), regular, regular((nz + 1,)),
+            pltpu.SMEM((picks, own_blocks), jnp.int32), vmem((n, snaps, width), F32),
+            vmem((2, width, snaps), F32), vmem((2, snaps, width), F32), vmem((width, snaps), F32),
+            vmem((3, n, 2, tile, width), BF16), vmem((2 * ns, tile, width), BF16),
+            sem((5,)), sem, sem, sem((2,)), sem((2,)), sem((2, pieces + 2)), sem((4,)), sem((2,)),
+            sem((6,)), sem((6,)), sem((2,)), regular, regular((nz + 1,)),
         ],
         compiler_params=pltpu.CompilerParams(collective_id=0, has_side_effects=True,
                                              vmem_limit_bytes=40 * 2**20),
@@ -343,7 +448,7 @@
         out_shape=tuple(pltpu.HBM(a.shape, a.dtype) for a in (weighted, modes, corr)),
         in_specs=[inside] * 3,
         out_specs=(hbm,) * 3,
-        scratch_shapes=[sem((10,))],
+        scratch_shapes=[sem((3,))],
         compiler_params=pltpu.CompilerParams(vmem_limit_bytes=2**20),
         name="deliver",
     )(*(pltpu.with_memory_space_constraint(a, pltpu.VMEM) for a in (weighted, modes, corr)))

time: 69.2 us -> 66.5 us (0.961)
  Pallas kernels: 68.4 us -> 65.7 us
    pallas_call x1, Pallas kernels: 66 us -> 63.3 us  [fast_shards(): pl.pallas_call(functools.partial(fused, n, ns, 1.0 / (total * ns)), out_s...]
where the time goes in v2:
time: 66.5 us; the launch traced here: 66.3 us
  Pallas kernels  65.7 us (99%)
    pallas_call x1, Pallas kernels, fast_shards(): pl.pallas_call(functools.partial(fused, n, ns, 1.0 / (total * ns)), out_s...  63.3 us
    pallas_call x1, Pallas kernels, fast_shards(): pl.pallas_call(deliver, out_shape=tuple((pltpu.HBM(a.shape, a.dtype) for...  2.38 us

profile of v2, /device:TPU:1, one launch (start us, length us, event | category | flops | bytes accessed | tf_op | source)
XLA Modules:
  0.0 66.3 jit_solution(5671667512991190391)
XLA Ops:
  0.6 63.3 %fused.1 = (bf16[4096,512]{1,0:T(8,128)(2,1)S(1)}, bf16[4096,128]{1,0:T(8,128)(2,1)S(1)}, f32[64,128]{1,0:T(8,128)S(1)}) custom-call(s32[3,32]{1,0:T(4,128)} %bitcast.4, bf16[128,128,128]{2,1,0:T(8,128)(2,1)} %bitcast.3, bf16[32,3,128,128]{3,2,1,0:T(8,128)(2,1)} %mass_hbm.1, bf16[512,128]{1,0:T(8,128)(2,1)} %eig_hbm.1), custom_call_target="tpu_custom_call" | custom-call | tf_op jit(solution)/shard_map/fused/pallas_call | solution.py:425
  63.9 2.4 %deliver.1 = (bf16[4096,512]{1,0:T(8,128)(2,1)}, bf16[4096,128]{1,0:T(8,128)(2,1)}, f32[64,128]{1,0:T(8,128)}) custom-call(bf16[4096,512]{1,0:T(8,128)(2,1)S(1)} %get-tuple-element.9.weighted, bf16[4096,128]{1,0:T(8,128)(2,1)S(1)} %get-tuple-element.10.modes, f32[64,128]{1,0:T(8,128)S(1)} %get-tuple-element.11.corr), custom_call_target="tpu_custom_call" | custom-call | tf_op jit(solution)/shard_map/deliver/pallas_call | solution.py:446

commit v3 on v2

--- a/solution.py
+++ b/solution.py
@@ -17,8 +17,8 @@
     return lax.dot_general(left, right, (((0,), (0,)), ((), ())), preferred_element_type=F32)
 
 
-def fused(n, ns, scale, near_hbm, src, mass_hbm, eig_hbm, weighted, modes, corr_out,
-          base, far, win, mass, eig, near, acc, late, given, given_late, tiles, recv,
+def fused(n, ns, near_hbm, src, mass_hbm, eig_hbm, weighted, modes, recv,
+          base, far, win, mass, eig, near, acc, late, given, given_late, tiles,
           loc, send_own, recv_own, recv_rim, send_far, recv_far, send_out, fwd_sems, give_sems, take_sems,
           tile_sems, gate, sync):
     nz = ns // 2
@@ -66,7 +66,8 @@
     barrier = pltpu.get_barrier_semaphore()
     hail(barrier)
     edge = c != y
-    outer = edge | ((y == 0) & (s > 0)) | ((y == 1) & (s < ns - 1))
+    cross_halo = jnp.logical_not(edge) & (((y == 0) & (s > 0)) | ((y == 1) & (s < ns - 1)))
+    outer = edge | cross_halo
     cross_rim = ((y == 0) & (s > 0)) | ((y == 1) & (s < ns - 1))
     plane_rim = ((y == 0) & (s < ns - 1)) | ((y == 1) & (s > 0))
 
@@ -78,19 +79,28 @@
     fetch_eig = local(3, eig_hbm, eig)
     fetch_near = local(4, near_hbm, near)
 
-    mains = []
-    for o in range(pieces):
-        for co in range(2):
-            at = yo * chip_blocks + ((pieces - 1 - o) * HB if co == 0 else own_blocks + o * HB)
-            to = (pieces - o) * HB if co == 0 else (1 + o) * HB
-            mains.append(remote(rows_of(at, HB), far.at[c, pl.ds(to, HB)], send_far.at[jnp.where((c == 0) & (o == pieces - 4), 1, 0)] if o == pieces - 4 else send_far.at[0],
-                                recv_far.at[c, o + 1], (s, 2 * yo + co)))
+    def main_copy(o, co):
+        at = yo * chip_blocks + jnp.where(co == 0, (pieces - 1 - o) * HB, own_blocks + o * HB)
+        to = jnp.where(co == 0, (pieces - o) * HB, (1 + o) * HB)
+        watched = jnp.where(c == 0, 1, 0) if o == pieces - 4 else 0
+        return remote(rows_of(at, HB), far.at[c, pl.ds(to, HB)], send_far.at[watched],
+                      recv_far.at[c, o + 1], (s, 2 * yo + co))
+
+    mains = [main_copy(0, yo)]
+    for o in range(1, pieces):
+        mains += [main_copy(o, yo), main_copy(o - 1, y)]
+    mains.append(main_copy(pieces - 1, y))
+
     def sent(count, i):
         rows = rows_of(0, count * HB)
         remote(rows, rows, send_far.at[i], recv_own, (s, partner)).wait_send()
 
-    cross_edge = remote(rows_of(chip_blocks - yo * HB, HB), far.at[c, pl.ds(y * top, HB)],
-                        send_out.at[0], recv_far.at[c, pieces + 1], (s, 2 * yo + y))
+    half_rim = HB // 2
+    edge_first = yo * half_rim
+    cross_edges = [
+        remote(rows_of(chip_blocks - yo * HB + at, half_rim), far.at[c, pl.ds(y * top + at, half_rim)],
+               send_out.at[4 * i], recv_far.at[c, pieces + 1 + i], (s, 2 * yo + y))
+        for i, at in enumerate((edge_first, half_rim - edge_first))]
     cross = remote(rows_of(y * (blocks - HB), HB), far.at[c, pl.ds(yo * top, HB)],
                    send_out.at[1], recv_far.at[c, pieces + 1], (s + 2 * y - 1, yo * (n - 1)))
     plane = remote(rows_of(yo * (blocks - HB), HB), base.at[c, pl.ds(y * top, HB)],
@@ -114,7 +124,8 @@
     def _():
         for copy in mains:
             copy.start()
-        cross_edge.start()
+        for copy in cross_edges:
+            copy.start()
 
     own.start()
     pl.when(jnp.logical_not(edge))(plane_edge.start)
@@ -124,9 +135,9 @@
     pl.when(plane_rim)(plane.start)
     pl.when(cross_rim & (c == 0))(cross.start)
 
-    def wait_rim(buffer, index, recvs):
-        remote(buffer.at[index, pl.ds(0, HB)], buffer.at[index, pl.ds(0, HB)], send_own, recvs,
-               (s, partner)).wait_recv()
+    def wait_rim(buffer, index, recvs, count=HB):
+        rows = buffer.at[index, pl.ds(0, count)]
+        remote(rows, rows, send_own, recvs, (s, partner)).wait_recv()
 
     def masses_of(row):
         return jnp.concatenate([mass[row, j] for j in range(picks)], axis=1)
@@ -205,8 +216,8 @@
     fetch.wait()
     fetch_near.wait()
 
-    def held(buffer, index, slot):
-        return buffer[index, pl.ds(pl.multiple_of(slot * HB, HB), HB)].reshape(rim, width)
+    def held(buffer, index, slot, first=0, count=HB):
+        return buffer[index, pl.ds(slot * HB + first, count)].reshape(count * size, width)
 
     def add(first, last, band, count, value):
         for i in range(count):
@@ -239,17 +250,18 @@
         lanes = lanes_far[index]
         known = 2 + index
 
-        def rows_at(order):
-            return pl.ds(pl.multiple_of((slot_of(order) - 1) * rim, rim), rim)
-
-        def admit(order):
-            first = pl.multiple_of(slot_of(order) * HB, HB)
-            win[pl.ds(first, HB)] = far[index, pl.ds(first, HB)]
-
-        def gathered(order, count):
+        def rows_at(order, first=0, count=HB):
+            at = (slot_of(order) - 1) * rim + first * size
+            return pl.ds(pl.multiple_of(at, size), count * size)
+
+        def admit(order, first=0, count=HB):
+            at = slot_of(order) * HB + first
+            win[pl.ds(at, count)] = far[index, pl.ds(at, count)]
+
+        def gathered(order, count, first=0, rows=HB):
             slot = slot_of(order)
-            parts = [held(base, 0, slot), held(base, 1, slot)]
-            return jnp.concatenate(parts + [held(far, i, slot) for i in range(count)], axis=1)
+            parts = [held(base, i, slot, first, rows) for i in range(2)]
+            return jnp.concatenate(parts + [held(far, i, slot, first, rows) for i in range(count)], axis=1)
 
         def meet(order):
             rows = rows_at(order)
@@ -265,16 +277,26 @@
             modes[rows_at(order), :] = jnp.dot(gathered(order, 2), vectors,
                                                preferred_element_type=F32).astype(BF16)
 
-        def work(order):
-            slot = slot_of(order)
-            for i in range(HB):
-                row = (slot - 1) * HB + i
+        def work(order, first=0, count=HB):
+            for i in range(count):
+                row = (slot_of(order) - 1) * HB + first + i
                 fields = jnp.concatenate([win[place_of(row, j)] for j in range(picks)], axis=0)
                 product = jnp.dot(masses_of(row), fields, preferred_element_type=F32)
                 weighted[pl.ds(pl.multiple_of(row * size, size), size), pl.ds(lanes, width)] = (
                     product.astype(BF16))
             late[index, :, 0:(known + 1) * width] += transposed_dot(
-                weighted[rows_at(order), pl.ds(lanes, width)], gathered(order, index + 1))
+                weighted[rows_at(order, first, count), pl.ds(lanes, width)],
+                gathered(order, index + 1, first, count))
+
+        def wait_outer():
+            @pl.when(edge)
+            def _():
+                for i in range(2):
+                    wait_rim(far, index, recv_far.at[index, pieces + 1 + i], half_rim)
+
+            @pl.when(cross_halo)
+            def _():
+                wait_rim(far, index, recv_far.at[index, pieces + 1])
 
         wait_rim(far, index, recv_far.at[index, 1])
         mid = far.at[index, pl.ds(slot_of(1) * HB, HB)]
@@ -309,7 +331,8 @@
                     pl.when(cross_rim)(cross.start)
                     for copy in mains:
                         copy.start()
-                    cross_edge.start()
+                    for copy in cross_edges:
+                        copy.start()
             work(p + 1)
 
         wait_rim(far, index, recv_far.at[index, pieces])
@@ -324,7 +347,7 @@
 
         if index == 0:
             finish()
-            pl.when(outer)(lambda: wait_rim(far, index, recv_far.at[index, pieces + 1]))
+            wait_outer()
             admit(pieces + 1)
             work(pieces)
             for j in range(known + 1):
@@ -338,31 +361,31 @@
 
         @pl.when(jnp.logical_not(edge))
         def _():
-            pl.when(outer)(lambda: wait_rim(far, index, recv_far.at[index, pieces + 1]))
+            pl.when(cross_halo)(lambda: wait_rim(far, index, recv_far.at[index, pieces + 1]))
             admit(pieces + 1)
             work(pieces)
             last_give.start()
 
-        finish()
-        pack_far_band(1, known, known + 1)
-        send_far_band(known, known + 1)
-
         @pl.when(edge)
         def _():
-            wait_rim(far, index, recv_far.at[index, pieces + 1])
-            admit(pieces + 1)
-            work(pieces)
+            for i, at in enumerate((y * half_rim, yo * half_rim)):
+                wait_rim(far, index, recv_far.at[index, pieces + 1 + i], half_rim)
+                admit(pieces + 1, at, half_rim)
+                work(pieces, at, half_rim)
             last_give.wait_recv()
             for t in range(n):
                 column = jnp.where(z < n // 2, n - 1 - t, t)
                 j = lax.rem(column, 2) + jnp.where(column // 2 == y, 0, 2)
                 lanes_of = pl.ds(pl.multiple_of(j * width, width), width)
-                value = (late[index, :, lanes_of] + given_late[:, lanes_of]).T
-                tiles[2, t] = value.astype(BF16).reshape(tiles.shape[2:])
+                value = (late[index, :, lanes_of] + given_late[:, lanes_of]).astype(BF16)
+                tiles[2, t] = value.T.reshape(tiles.shape[2:])
                 for half in range(2):
                     remote(tiles.at[2, t, half], recv.at[ns + s], tile_sems.at[0], tile_sems.at[1],
                            (2 * column + half, 2 * yo + 1)).start()
 
+        finish()
+        pack_far_band(1, known, known + 1)
+        send_far_band(known, known + 1)
         project(pieces)
         forward.wait_send()
         pl.when(jnp.logical_not(edge))(last_give.wait_send)
@@ -372,7 +395,8 @@
 
     pl.when(c == 0)(lambda: sent(2 * pieces - 2, 0))
     pl.when(c == 1)(lambda: sent(2 * pieces, 0))
-    cross_edge.wait_send()
+    for copy in cross_edges:
+        copy.wait_send()
     own.wait_send()
     pl.when(jnp.logical_not(edge))(plane_edge.wait_send)
     pl.when(plane_rim)(plane.wait_send)
@@ -391,17 +415,18 @@
     pl.when(edge)(tile_bytes.wait_send)
     all_tiles = recv.at[pl.ds(0, 2 * ns - 1)]
     remote(all_tiles, all_tiles, tile_sems.at[0], tile_sems.at[1], (s, partner)).wait_recv()
-    total = recv[0].astype(F32)
-    for i in range(1, 2 * ns):
-        total = total + recv[i].astype(F32)
-    corr_out[...] = total * scale
-
-
-def deliver(weighted, modes, corr, weighted_out, modes_out, corr_out, sems):
+
+
+def deliver(scale, weighted, modes, parts, weighted_out, modes_out, corr_out, corr, sems):
     pairs = ((weighted, weighted_out), (modes, modes_out), (corr, corr_out))
     copies = [pltpu.make_async_copy(held, target, sems.at[i]) for i, (held, target) in enumerate(pairs)]
-    for copy in copies:
+    for copy in copies[:2]:
         copy.start()
+    total = parts[0].astype(F32)
+    for i in range(1, parts.shape[0]):
+        total = total + parts[i].astype(F32)
+    corr[...] = total * scale
+    copies[2].start()
     for copy in copies:
         copy.wait()
 
@@ -422,11 +447,11 @@
     hbm = pl.BlockSpec(memory_space=pltpu.HBM)
     inside = pl.BlockSpec(memory_space=pltpu.VMEM)
     block = (size, width)
-    weighted, modes, corr = pl.pallas_call(
-        functools.partial(fused, n, ns, 1.0 / (total * ns)),
+    weighted, modes, parts = pl.pallas_call(
+        functools.partial(fused, n, ns),
         out_shape=(jax.ShapeDtypeStruct((rows, snaps), BF16),
                    jax.ShapeDtypeStruct((rows, modes_count), BF16),
-                   jax.ShapeDtypeStruct((tile, width), F32)),
+                   jax.ShapeDtypeStruct((2 * ns, tile, width), BF16)),
         in_specs=[hbm] * 4,
         out_specs=(inside, inside, inside),
         scratch_shapes=[
@@ -434,8 +459,8 @@
             vmem(mass_blocks.shape, BF16), vmem(eigvecs.shape, BF16),
             pltpu.SMEM((picks, own_blocks), jnp.int32), vmem((n, snaps, width), F32),
             vmem((2, width, snaps), F32), vmem((2, snaps, width), F32), vmem((width, snaps), F32),
-            vmem((3, n, 2, tile, width), BF16), vmem((2 * ns, tile, width), BF16),
-            sem((5,)), sem, sem, sem((2,)), sem((2,)), sem((2, pieces + 2)), sem((4,)), sem((2,)),
+            vmem((3, n, 2, tile, width), BF16),
+            sem((5,)), sem, sem, sem((2,)), sem((2,)), sem((2, pieces + 3)), sem((5,)), sem((2,)),
             sem((6,)), sem((6,)), sem((2,)), regular, regular((nz + 1,)),
         ],
         compiler_params=pltpu.CompilerParams(collective_id=0, has_side_effects=True,
@@ -444,14 +469,14 @@
     )(*(pltpu.with_memory_space_constraint(a, pltpu.HBM) for a in (
         neighbours.T, snapshots.reshape(total // size, size, width), mass_blocks, eigvecs)))
     weighted, modes, corr = pl.pallas_call(
-        deliver,
-        out_shape=tuple(pltpu.HBM(a.shape, a.dtype) for a in (weighted, modes, corr)),
+        functools.partial(deliver, 1.0 / (total * ns)),
+        out_shape=(pltpu.HBM(weighted.shape, BF16), pltpu.HBM(modes.shape, BF16), pltpu.HBM((tile, width), F32)),
         in_specs=[inside] * 3,
         out_specs=(hbm,) * 3,
-        scratch_shapes=[sem((3,))],
+        scratch_shapes=[vmem((tile, width), F32), sem((3,))],
         compiler_params=pltpu.CompilerParams(vmem_limit_bytes=2**20),
         name="deliver",
-    )(*(pltpu.with_memory_space_constraint(a, pltpu.VMEM) for a in (weighted, modes, corr)))
+    )(*(pltpu.with_memory_space_constraint(a, pltpu.VMEM) for a in (weighted, modes, parts)))
     return weighted, corr.T, modes
 
 

time: 66.5 us -> 66 us (level)
  no operation moved by 1% of the time
where the time goes in v3:
time: 66 us; the launch traced here: 65.7 us
  Pallas kernels  65.1 us (99%)
    pallas_call x1, Pallas kernels, fast_shards(): pl.pallas_call(functools.partial(fused, n, ns), out_shape=(jax.ShapeDtype...  62.7 us
    pallas_call x1, Pallas kernels, fast_shards(): pl.pallas_call(functools.partial(deliver, 1.0 / (total * ns)), out_shape=...  2.38 us

profile of v3, /device:TPU:1, one launch (start us, length us, event | category | flops | bytes accessed | tf_op | source)
XLA Modules:
  0.0 65.7 jit_solution(11818274240763041210)
XLA Ops:
  0.6 62.7 %fused.1 = (bf16[4096,512]{1,0:T(8,128)(2,1)S(1)}, bf16[4096,128]{1,0:T(8,128)(2,1)S(1)}, bf16[16,64,128]{2,1,0:T(8,128)(2,1)S(1)}) custom-call(s32[3,32]{1,0:T(4,128)} %bitcast.4, bf16[128,128,128]{2,1,0:T(8,128)(2,1)} %bitcast.3, bf16[32,3,128,128]{3,2,1,0:T(8,128)(2,1)} %mass_hbm.1, bf16[512,128]{1,0:T(8,128)(2,1)} %eig_hbm.1), custom_call_target="tpu_custom_call" | custom-call | tf_op jit(solution)/shard_map/fused/pallas_call | solution.py:450
  63.3 2.4 %deliver.1 = (bf16[4096,512]{1,0:T(8,128)(2,1)}, bf16[4096,128]{1,0:T(8,128)(2,1)}, f32[64,128]{1,0:T(8,128)}) custom-call(bf16[4096,512]{1,0:T(8,128)(2,1)S(1)} %get-tuple-element.9.weighted, bf16[4096,128]{1,0:T(8,128)(2,1)S(1)} %get-tuple-element.10.modes, bf16[16,64,128]{2,1,0:T(8,128)(2,1)S(1)} %get-tuple-element.11.parts), custom_call_target="tpu_custom_call" | custom-call | tf_op jit(solution)/shard_map/deliver/pallas_call | solution.py:471

commit v4 on v3

--- a/solution.py
+++ b/solution.py
@@ -99,13 +99,13 @@
     edge_first = yo * half_rim
     cross_edges = [
         remote(rows_of(chip_blocks - yo * HB + at, half_rim), far.at[c, pl.ds(y * top + at, half_rim)],
-               send_out.at[4 * i], recv_far.at[c, pieces + 1 + i], (s, 2 * yo + y))
+               send_far.at[0], recv_far.at[c, pieces + 1 + i], (s, 2 * yo + y))
         for i, at in enumerate((edge_first, half_rim - edge_first))]
     cross = remote(rows_of(y * (blocks - HB), HB), far.at[c, pl.ds(yo * top, HB)],
-                   send_out.at[1], recv_far.at[c, pieces + 1], (s + 2 * y - 1, yo * (n - 1)))
+                   send_out.at[0], recv_far.at[c, pieces + 1], (s + 2 * y - 1, yo * (n - 1)))
     plane = remote(rows_of(yo * (blocks - HB), HB), base.at[c, pl.ds(y * top, HB)],
-                   send_out.at[2], recv_rim.at[c], (s + 1 - 2 * y, y * (n - 1)))
-    plane_edge = remote(edge_rows, base.at[c, pl.ds(yo * top, HB)], send_out.at[3], recv_rim.at[c],
+                   send_out.at[1], recv_rim.at[c], (s + 1 - 2 * y, y * (n - 1)))
+    plane_edge = remote(edge_rows, base.at[c, pl.ds(yo * top, HB)], send_out.at[2], recv_rim.at[c],
                         (s, partner))
     own = remote(rows_of(y * chip_blocks + (1 - c) * (own_blocks - HB), own_blocks + HB),
                  base.at[c, pl.ds(c * HB, own_blocks + HB)], send_own, recv_own, (s, partner))
@@ -129,7 +129,7 @@
 
     own.start()
     pl.when(jnp.logical_not(edge))(plane_edge.start)
-    for i in range(nz + 1):
+    for i in range(nz):
         hail(sync.at[i])
         heed(sync.at[i])
     pl.when(plane_rim)(plane.start)
@@ -393,10 +393,8 @@
     phase(0)
     phase(1)
 
-    pl.when(c == 0)(lambda: sent(2 * pieces - 2, 0))
-    pl.when(c == 1)(lambda: sent(2 * pieces, 0))
-    for copy in cross_edges:
-        copy.wait_send()
+    pl.when(c == 0)(lambda: sent(2 * pieces - 1, 0))
+    pl.when(c == 1)(lambda: sent(2 * pieces + 1, 0))
     own.wait_send()
     pl.when(jnp.logical_not(edge))(plane_edge.wait_send)
     pl.when(plane_rim)(plane.wait_send)
@@ -460,8 +458,8 @@
             pltpu.SMEM((picks, own_blocks), jnp.int32), vmem((n, snaps, width), F32),
             vmem((2, width, snaps), F32), vmem((2, snaps, width), F32), vmem((width, snaps), F32),
             vmem((3, n, 2, tile, width), BF16),
-            sem((5,)), sem, sem, sem((2,)), sem((2,)), sem((2, pieces + 3)), sem((5,)), sem((2,)),
-            sem((6,)), sem((6,)), sem((2,)), regular, regular((nz + 1,)),
+            sem((5,)), sem, sem, sem((2,)), sem((2,)), sem((2, pieces + 3)), sem((3,)), sem((2,)),
+            sem((6,)), sem((6,)), sem((2,)), regular, regular((nz,)),
         ],
         compiler_params=pltpu.CompilerParams(collective_id=0, has_side_effects=True,
                                              vmem_limit_bytes=40 * 2**20),

time: 66 us -> 66 us (level)
  no operation moved by 1% of the time
where the time goes in v4:
time: 66 us; the launch traced here: 65.7 us
  Pallas kernels  65 us (98%)
    pallas_call x1, Pallas kernels, fast_shards(): pl.pallas_call(functools.partial(fused, n, ns), out_shape=(jax.ShapeDtype...  62.7 us
    pallas_call x1, Pallas kernels, fast_shards(): pl.pallas_call(functools.partial(deliver, 1.0 / (total * ns)), out_shape=...  2.38 us

profile of v4, /device:TPU:1, one launch (start us, length us, event | category | flops | bytes accessed | tf_op | source)
XLA Modules:
  0.0 65.7 jit_solution(7407378181681796980)
XLA Ops:
  0.6 62.7 %fused.1 = (bf16[4096,512]{1,0:T(8,128)(2,1)S(1)}, bf16[4096,128]{1,0:T(8,128)(2,1)S(1)}, bf16[16,64,128]{2,1,0:T(8,128)(2,1)S(1)}) custom-call(s32[3,32]{1,0:T(4,128)} %bitcast.4, bf16[128,128,128]{2,1,0:T(8,128)(2,1)} %bitcast.3, bf16[32,3,128,128]{3,2,1,0:T(8,128)(2,1)} %mass_hbm.1, bf16[512,128]{1,0:T(8,128)(2,1)} %eig_hbm.1), custom_call_target="tpu_custom_call" | custom-call | tf_op jit(solution)/shard_map/fused/pallas_call | solution.py:448
  63.3 2.4 %deliver.1 = (bf16[4096,512]{1,0:T(8,128)(2,1)}, bf16[4096,128]{1,0:T(8,128)(2,1)}, f32[64,128]{1,0:T(8,128)}) custom-call(bf16[4096,512]{1,0:T(8,128)(2,1)S(1)} %get-tuple-element.9.weighted, bf16[4096,128]{1,0:T(8,128)(2,1)S(1)} %get-tuple-element.10.modes, bf16[16,64,128]{2,1,0:T(8,128)(2,1)S(1)} %get-tuple-element.11.parts), custom_call_target="tpu_custom_call" | custom-call | tf_op jit(solution)/shard_map/deliver/pallas_call | solution.py:469
